TPU v7x, 32 devices: a whole 2x2x4 slice. The times are simulated.
32 devices in a mesh: seq: 4 (over y, core), dp: 8 (over z, x).
Axes of the slice: x: 2, y: 2, z: 4, core: 2. Of those that a mesh axis runs over, the one named last changes fastest.
Arguments:
- tokens: bfloat16 [16, 1024, 1024], P('dp', 'seq'), may hold values from -6 to 6
- cotangent: bfloat16 [16, 1024, 1024], P('dp', 'seq'), may hold values from -6 to 6
- row_lengths: int32 [16], P('dp'), may hold values from 512 to 1024
- source_lengths: int32 [16], P('dp'), may hold values from 30 to 400
- first_gain: float32 [1024], replicated, may hold values from 0.1 to 1.9
- first_shift: float32 [1024], replicated, may hold values from -2 to 2
- attend_weight: bfloat16 [1024, 3072], replicated, may hold values from -0.25 to 0.25
- attend_bias: float32 [3072], replicated, may hold values from -2 to 2
- output_weight: bfloat16 [1024, 1024], replicated, may hold values from -0.75 to 0.75
- output_bias: float32 [1024], replicated, may hold values from -2 to 2
- second_gain: float32 [1024], replicated, may hold values from 0.1 to 1.9
- second_shift: float32 [1024], replicated, may hold values from -2 to 2
- expand_weight: bfloat16 [1024, 4096], replicated, may hold values from -0.1875 to 0.1875
- expand_bias: float32 [4096], replicated, may hold values from -2 to 2
- contract_weight: bfloat16 [4096, 1024], replicated, may hold values from -0.09375 to 0.09375
- contract_bias: float32 [1024], replicated, may hold values from -2 to 2
- prefix_table: bfloat16 [10, 1024], replicated, may hold values from -6 to 6
- lift_weight: bfloat16 [1024, 512], replicated, may hold values from -0.1875 to 0.1875
- lift_bias: float32 [512], replicated, may hold values from -2 to 2
- fan_weight: bfloat16 [512, 2048], replicated, may hold values from -0.375 to 0.375
- fan_bias: float32 [2048], replicated, may hold values from -2 to 2
Outputs:
- activations: bfloat16 [16, 1024, 1024], P('dp', 'seq')
- input_grad: float32 [16, 1024, 1024], P('dp', 'seq')
- grad_table: float32 [10, 1024], replicated
- grad_lift: float32 [1024, 512], replicated
- grad_liftbias: float32 [512], replicated
- grad_fan: float32 [512, 2048], replicated
- grad_fanbias: float32 [2048], replicated
All inputs are finite; a program needn't handle non-finite values.
Results may differ from a plain program's by a relative error of at most 0.025.
Values may be sent and summed in bfloat16 or wider, within the bound.
No kernel may reach another device: no remote copies, remote signals or barrier semaphores. Data moves between devices by JAX's collectives and lax.ppermute only.
A program may use at most 320 MiB of HBM per device.

v0:
```python
import jax
import jax.numpy as jnp
from jax import lax
from jax.sharding import PartitionSpec as P

D = 1024
HEADS = 16
HEAD_DIM = 64
PREFIX = 10
best_precision = lax.Precision.HIGHEST


def layer_norm(values, norm_gain, norm_shift):
    centred = values - jnp.mean(values, axis=-1, keepdims=True)
    variance = jnp.mean(centred * centred, axis=-1, keepdims=True)
    return centred * lax.rsqrt(variance + 1e-05) * norm_gain + norm_shift


def gelu_tanh(values):
    return jax.nn.gelu(values, approximate=True)


def block_forward(tokens, row_lengths, frozen, prefix_keyval, again):
    (
        first_gain,
        first_shift,
        attend_weight,
        attend_bias,
        output_weight,
        output_bias,
        second_gain,
        second_shift,
        expand_weight,
        expand_bias,
        contract_weight,
        contract_bias,
    ) = frozen
    row_count = tokens.shape[0]
    tok_count = tokens.shape[1]
    inputs = tokens.astype(jnp.float32)
    normed = layer_norm(inputs, first_gain, first_shift).astype(jnp.bfloat16)
    project = jnp.dot(normed, attend_weight, preferred_element_type=jnp.float32) + attend_bias
    queries = project[..., :D].astype(jnp.bfloat16).reshape(row_count, tok_count, HEADS, HEAD_DIM)
    local_keyval = project[..., D:].astype(jnp.bfloat16)
    if again:
        row_keyval = lax.all_gather(local_keyval, "seq", axis=1, tiled=True)
    else:
        row_keyval = lax.all_gather(local_keyval, "seq", axis=1, tiled=True)
    seq_total = row_keyval.shape[1]
    row_keys = row_keyval[..., :D].reshape(row_count, seq_total, HEADS, HEAD_DIM)
    row_values = row_keyval[..., D:].reshape(row_count, seq_total, HEADS, HEAD_DIM)
    prefix_keys = prefix_keyval[:, :D].reshape(PREFIX, HEADS, HEAD_DIM)
    prefix_values = prefix_keyval[:, D:].reshape(PREFIX, HEADS, HEAD_DIM)
    scores = (
        jnp.einsum("rqhd,rkhd->rhqk", queries, row_keys, preferred_element_type=jnp.float32) * 0.125
    )
    prefix_scores = (
        jnp.einsum("rqhd,phd->rhqp", queries, prefix_keys, preferred_element_type=jnp.float32)
        * 0.125
    )
    query_places = lax.axis_index("seq") * tok_count + jnp.arange(tok_count)
    key_places = jnp.arange(seq_total)
    visible = (key_places[None, None, :] <= query_places[None, :, None]) & (
        key_places[None, None, :] < row_lengths[:, None, None]
    )
    scores = jnp.where(visible[:, None], scores, -jnp.inf)
    highest = jnp.maximum(
        jnp.max(scores, axis=-1, keepdims=True), jnp.max(prefix_scores, axis=-1, keepdims=True)
    )
    denominator = jnp.sum(jnp.exp(scores - highest), axis=-1, keepdims=True) + jnp.sum(
        jnp.exp(prefix_scores - highest), axis=-1, keepdims=True
    )
    log_total = highest + jnp.log(denominator)
    weights = jnp.exp(scores - log_total)
    prefix_weights = jnp.exp(prefix_scores - log_total)
    rounded = weights.astype(jnp.bfloat16)
    prefix_rounded = prefix_weights.astype(jnp.bfloat16)
    attended = jnp.einsum(
        "rhqk,rkhd->rqhd", rounded, row_values, preferred_element_type=jnp.float32
    )
    attended = attended + jnp.einsum(
        "rhqp,phd->rqhd", prefix_rounded, prefix_values, preferred_element_type=jnp.float32
    )
    mixed_heads = attended.reshape(row_count, tok_count, D).astype(jnp.bfloat16)
    residual = (
        inputs
        + jnp.dot(mixed_heads, output_weight, preferred_element_type=jnp.float32)
        + output_bias
    )
    normed_two = layer_norm(residual, second_gain, second_shift).astype(jnp.bfloat16)
    expanded = jnp.dot(normed_two, expand_weight, preferred_element_type=jnp.float32) + expand_bias
    activated = gelu_tanh(expanded).astype(jnp.bfloat16)
    result = (
        residual
        + jnp.dot(activated, contract_weight, preferred_element_type=jnp.float32)
        + contract_bias
    )
    return (
        inputs,
        queries,
        row_keys,
        row_values,
        prefix_keys,
        prefix_values,
        weights,
        prefix_weights,
        rounded,
        prefix_rounded,
        residual,
        expanded,
        result,
        log_total,
    )


def prefix_grads(prefix_grad, prefix_table, lift_weight, fan_weight, lifted, lifted_low):
    grad_fanbias = jnp.sum(prefix_grad, axis=0)
    grad_fan = jnp.dot(lifted_low.astype(jnp.float32).T, prefix_grad, precision=best_precision)
    grad_lifted = jnp.dot(
        prefix_grad, fan_weight.astype(jnp.float32).T, precision=best_precision
    ) * (1.0 - lifted * lifted)
    grad_liftbias = jnp.sum(grad_lifted, axis=0)
    grad_lift = jnp.dot(prefix_table.astype(jnp.float32).T, grad_lifted, precision=best_precision)
    grad_table = jnp.dot(grad_lifted, lift_weight.astype(jnp.float32).T, precision=best_precision)
    return (grad_table, grad_lift, grad_liftbias, grad_fan, grad_fanbias)


def per_device(
    tokens,
    cotangent,
    row_lengths,
    source_lengths,
    first_gain,
    first_shift,
    attend_weight,
    attend_bias,
    output_weight,
    output_bias,
    second_gain,
    second_shift,
    expand_weight,
    expand_bias,
    contract_weight,
    contract_bias,
    prefix_table,
    lift_weight,
    lift_bias,
    fan_weight,
    fan_bias,
):
    frozen = (
        first_gain,
        first_shift,
        attend_weight,
        attend_bias,
        output_weight,
        output_bias,
        second_gain,
        second_shift,
        expand_weight,
        expand_bias,
        contract_weight,
        contract_bias,
    )
    lifted = jnp.tanh(
        jnp.dot(prefix_table, lift_weight, preferred_element_type=jnp.float32) + lift_bias
    )
    lifted_low = lifted.astype(jnp.bfloat16)
    prefix_keyval = (
        jnp.dot(lifted_low, fan_weight, preferred_element_type=jnp.float32) + fan_bias
    ).astype(jnp.bfloat16)
    state = block_forward(tokens, row_lengths, frozen, prefix_keyval, False)
    activations = state[12].astype(jnp.bfloat16)
    again_tokens = lax.optimization_barrier((tokens, activations))[0]
    state = block_forward(again_tokens, row_lengths, frozen, prefix_keyval, True)
    (
        inputs,
        queries,
        row_keys,
        row_values,
        prefix_keys,
        prefix_values,
        weights,
        prefix_weights,
        rounded,
        prefix_rounded,
        residual,
        expanded,
        result,
        log_total,
    ) = state
    row_count = tokens.shape[0]
    tok_count = tokens.shape[1]
    places = lax.axis_index("seq") * tok_count + jnp.arange(tok_count)
    target = (places[None, :] >= source_lengths[:, None]) & (places[None, :] < row_lengths[:, None])
    grad_out = jnp.where(target[..., None], cotangent, jnp.zeros_like(cotangent))
    grad_hidden = jnp.einsum(
        "rcd,fd->rcf", grad_out, contract_weight, preferred_element_type=jnp.float32
    )
    _, gelu_back = jax.vjp(gelu_tanh, expanded)
    grad_expand = gelu_back(grad_hidden)[0].astype(jnp.bfloat16)
    grad_normed = jnp.einsum(
        "rcf,df->rcd", grad_expand, expand_weight, preferred_element_type=jnp.float32
    )
    _, second_back = jax.vjp(lambda values: layer_norm(values, second_gain, second_shift), residual)
    grad_residual = grad_out.astype(jnp.float32) + second_back(grad_normed)[0]
    grad_mixed = jnp.einsum(
        "rcd,ed->rce",
        grad_residual.astype(jnp.bfloat16),
        output_weight,
        preferred_element_type=jnp.float32,
    )
    grad_heads = grad_mixed.astype(jnp.bfloat16).reshape(row_count, tok_count, HEADS, HEAD_DIM)
    grad_weights = jnp.einsum(
        "rqhd,rkhd->rhqk", grad_heads, row_values, preferred_element_type=jnp.float32
    )
    grad_preweights = jnp.einsum(
        "rqhd,phd->rhqp", grad_heads, prefix_values, preferred_element_type=jnp.float32
    )
    inner_sum = jnp.sum(weights * grad_weights, axis=-1, keepdims=True) + jnp.sum(
        prefix_weights * grad_preweights, axis=-1, keepdims=True
    )
    grad_scores = (weights * (grad_weights - inner_sum)).astype(jnp.bfloat16)
    grad_prescores = (prefix_weights * (grad_preweights - inner_sum)).astype(jnp.bfloat16)
    grad_queries = jnp.einsum(
        "rhqk,rkhd->rqhd", grad_scores, row_keys, preferred_element_type=jnp.float32
    )
    grad_queries = (
        grad_queries
        + jnp.einsum(
            "rhqp,phd->rqhd", grad_prescores, prefix_keys, preferred_element_type=jnp.float32
        )
    ) * 0.125
    grad_keys = (
        jnp.einsum("rhqk,rqhd->krhd", grad_scores, queries, preferred_element_type=jnp.float32)
        * 0.125
    )
    grad_values = jnp.einsum(
        "rhqk,rqhd->krhd", rounded, grad_heads, preferred_element_type=jnp.float32
    )
    owned = lax.psum_scatter(
        jnp.concatenate(
            [
                grad_keys.reshape(tok_count * lax.axis_size("seq"), row_count, D),
                grad_values.reshape(tok_count * lax.axis_size("seq"), row_count, D),
            ],
            axis=-1,
        ).astype(jnp.bfloat16),
        "seq",
        scatter_dimension=0,
        tiled=True,
    ).astype(jnp.float32)
    grad_owned = jnp.transpose(owned, (1, 0, 2)).astype(jnp.bfloat16)
    grad_prekeys = (
        jnp.einsum("rhqp,rqhd->phd", grad_prescores, queries, preferred_element_type=jnp.float32)
        * 0.125
    )
    grad_prevalues = jnp.einsum(
        "rhqp,rqhd->phd", prefix_rounded, grad_heads, preferred_element_type=jnp.float32
    )
    prefix_grad = jnp.concatenate(
        [grad_prekeys.reshape(PREFIX, D), grad_prevalues.reshape(PREFIX, D)], axis=-1
    )
    grad_project = jnp.concatenate(
        [grad_queries.reshape(row_count, tok_count, D).astype(jnp.bfloat16), grad_owned], axis=-1
    )
    grad_first = jnp.einsum(
        "rcf,df->rcd", grad_project, attend_weight, preferred_element_type=jnp.float32
    )
    _, first_back = jax.vjp(lambda values: layer_norm(values, first_gain, first_shift), inputs)
    input_grad = grad_residual + first_back(grad_first)[0]
    grad_table, grad_lift, grad_liftbias, grad_fan, grad_fanbias = prefix_grads(
        prefix_grad, prefix_table, lift_weight, fan_weight, lifted, lifted_low
    )
    grad_table, grad_lift, grad_liftbias, grad_fan, grad_fanbias = lax.psum(
        (grad_table, grad_lift, grad_liftbias, grad_fan, grad_fanbias), ("seq", "dp")
    )
    return (activations, input_grad, grad_table, grad_lift, grad_liftbias, grad_fan, grad_fanbias)


def solution(mesh):
    return jax.shard_map(
        per_device,
        mesh=mesh,
        in_specs=(
            P("dp", "seq", None),
            P("dp", "seq", None),
            P("dp"),
            P("dp"),
            P(),
            P(),
            P(),
            P(),
            P(),
            P(),
            P(),
            P(),
            P(),
            P(),
            P(),
            P(),
            P(),
            P(),
            P(),
            P(),
            P(),
        ),
        out_specs=(P("dp", "seq", None), P("dp", "seq", None), P(), P(), P(), P(), P()),
        check_vma=False,
    )
```

profile of v0, /device:TPU:0, one launch (start us, length us, event | category | flops | bytes accessed | tf_op | source)
XLA Modules:
  0.0 668.7 jit_solution(5564932534469927278)
XLA Ops:
  10.5 6.6 add_convert_fusion.1
  28.7 52.7 %all-gather.3.cloned.1.call-done = bf16[2,1024,2048]{2,1,0:T(8,128)(2,1)} async-done(((bf16[2,256,2048]{2,1,0:T(8,128)(2,1)}), bf16[2,1024,2048]{2,1,0:T(8,128)(2,1)}) %all-gather.3.cloned.1.call-update) | async-done | bytes 8388624 | tf_op jit(solution)/shard_map/all_gather | solution.py:48
  81.4 6.0 fusion.174
  87.4 6.2 copy.171
  93.6 6.2 copy.173
  99.8 15.9 %fusion = (f32[2,16,256]{2,1,0:T(8,128)S(1)}, f32[2,16,256,1024]{3,2,1,0:T(8,128)}) fusion(pred[2,256,1024]{2,1,0:T(8,128)(4,1)S(1)} %broadcast_and_fusion, bf16[2,256,16,64]{1,3,2,0:T(8,128)(2,1)} %bitcast.197, bf16[2,1024,16,64]{1,3,2,0:T(8,128)(2,1)} %bitcast.195), kind=kOutput, calls=%fused_computation.8 | convolution fusion | flops 1098899456 | bytes 39354368 | tf_op jit(solution)/shard_map/rqhd,rkhd->rhqk/dot_general | solution.py:55
  116.0 14.9 %exponential_reduce_fusion.1 = f32[2,16,256]{2,1,0:T(8,128)S(1)} fusion(f32[2,16,256,1024]{3,2,1,0:T(8,128)} %get-tuple-element.60, f32[2,16,256]{2,1,0:T(8,128)S(1)} %max.22, pred[2,256,1024]{2,1,0:T(8,128)(4,1)S(1)} %broadcast_and_fusion), kind=kLoop, calls=%fused_computation.6 | loop fusion | flops 33546240 | bytes 34144256 | tf_op jit(solution)/shard_map/reduce_sum | solution.py:70
  132.9 17.5 %fusion.74 = bf16[2,256,16,64]{1,3,2,0:T(8,128)(2,1)} fusion(f32[16,64,2,256]{3,1,0,2:T(8,128)} %fusion.137, bf16[2,1024,16,64]{1,3,2,0:T(8,128)(2,1)} %bitcast.198, f32[2,16,256,1024]{3,2,1,0:T(8,128)} %get-tuple-element.60, f32[2,16,256]{2,1,0:T(8,128)S(1)} %log_add_fusion.1, pred[2,256,1024]{2,1,0:T(8,128)(4,1)} %copy-done.2), kind=kOutput, calls=%fused_computation.94 | convolution fusion | flops 1108344832 | bytes 41451520 | tf_op jit(solution)/shard_map/rhqk,rkhd->rqhd/dot_general | solution.py:78
  153.7 10.4 %fusion.19 = bf16[2,256,4096]{2,1,0:T(8,128)(2,1)S(1)} fusion(bf16[1024,4096]{1,0:T(8,128)(2,1)} %param.33, f32[4096]{0:T(1024)S(1)} %copy-done.45, f32[2,256,1024]{2,1,0:T(8,128)S(1)} %get-tuple-element.62, f32[1024]{0:T(1024)S(1)} %copy-done.49, f32[1024]{0:T(1024)S(1)} %copy-done.38, f32[2,256]{1,0:T(2,128)S(1)} %add_rsqrt_fusion, ...), kind=kOutput, calls=%fused_computation.30 | convolution fusion | flops 4318560256 | bytes 14708736 | tf_op jit(solution)/shard_map/dot_general | solution.py:91
  164.2 5.5 add_convert_fusion.3
  170.5 4.0 add_convert_fusion
  177.8 12.7 %fusion.20 = f32[2,256,4096]{2,1,0:T(8,128)} fusion(bf16[4096,1024]{1,0:T(8,128)(2,1)} %param.35, bf16[2,256,1024]{2,1,0:T(8,128)(2,1)} %param.22, pred[2,256]{1,0:T(4,128)(4,1)S(1)} %compare_and_fusion), kind=kOutput, calls=%fused_computation.32 | convolution fusion | flops 4295491584 | bytes 17826304 | tf_op jit(solution)/shard_map/rcd,fd->rcf/dot_general | solution.py:197
  197.0 39.1 %all-gather.5.cloned.1.call-done = bf16[2,1024,2048]{2,1,0:T(8,128)(2,1)} async-done(((bf16[2,256,2048]{2,1,0:T(8,128)(2,1)}), bf16[2,1024,2048]{2,1,0:T(8,128)(2,1)}) %all-gather.5.cloned.1.call-update) | async-done | bytes 8388624 | tf_op jit(solution)/shard_map/all_gather | solution.py:46
  236.2 6.0 fusion.173
  242.2 6.2 copy.186
  248.4 6.2 copy.184
  254.6 15.9 %fusion.1 = (f32[2,16,256]{2,1,0:T(8,128)S(1)}, f32[2,16,256,1024]{3,2,1,0:T(8,128)}) fusion(pred[2,256,1024]{2,1,0:T(8,128)(4,1)} %copy-done.2, bf16[2,256,16,64]{1,3,2,0:T(8,128)(2,1)} %bitcast.185, bf16[2,1024,16,64]{1,3,2,0:T(8,128)(2,1)} %bitcast.182), kind=kOutput, calls=%fused_computation.9 | convolution fusion | flops 1098899456 | bytes 39354368 | tf_op jit(solution)/shard_map/rqhd,rkhd->rhqk/dot_general | solution.py:55
  270.5 14.9 %exponential_reduce_fusion = f32[2,16,256]{2,1,0:T(8,128)S(1)} fusion(f32[2,16,256,1024]{3,2,1,0:T(8,128)} %get-tuple-element.64, f32[2,16,256]{2,1,0:T(8,128)S(1)} %max.23, pred[2,256,1024]{2,1,0:T(8,128)(4,1)S(1)} %copy-done.3), kind=kLoop, calls=%fused_computation.3 | loop fusion | flops 33546240 | bytes 34144256 | tf_op jit(solution)/shard_map/reduce_sum | solution.py:70
  286.2 17.0 %fusion.141 = f32[2,16,64,256]{3,2,1,0:T(8,128)} fusion(bf16[2,1024,16,64]{1,3,2,0:T(8,128)(2,1)} %bitcast.188, f32[2,16,256,1024]{3,2,1,0:T(8,128)} %get-tuple-element.64, f32[2,16,256]{2,1,0:T(8,128)S(1)} %log_add_fusion, pred[2,256,1024]{2,1,0:T(8,128)(4,1)} %copy-done.2), kind=kOutput, calls=%fused_computation.169 | convolution fusion | flops 1107296256 | bytes 40402944 | tf_op jit(solution)/shard_map/rhqk,rkhd->rqhd/dot_general | solution.py:78
  309.0 23.9 %multiply_reduce_fusion.1 = (f32[2,256]{1,0:T(2,128)}, f32[2,256,1024]{2,1,0:T(8,128)}) fusion(f32[2,256,1024]{2,1,0:T(8,128)} %copy-done.4, f32[2,256]{1,0:T(2,128)S(1)} %broadcast_multiply_fusion, f32[1024]{0:T(1024)} %param.31, bf16[1024,4096]{1,0:T(8,128)(2,1)} %param.33, f32[2,256,4096]{2,1,0:T(8,128)} %fusion.20, f32[4096]{0:T(1024)} %param.34, ...), kind=kOutput, calls=%fused_computation.97 | convolution fusion | flops 8638693376 | bytes 21002240 | tf_op jit(solution)/shard_map/rcf,df->rcd/dot_general | solution.py:202
  344.1 27.3 %multiply_reduce_fusion = (f32[2,16,256]{2,1,0:T(8,128)}, f32[2,16,256,1024]{3,2,1,0:T(8,128)}) fusion(f32[2,16,256,1024]{3,2,1,0:T(8,128)} %get-tuple-element.64, f32[2,16,256]{2,1,0:T(8,128)S(1)} %log_add_fusion, pred[2,256,1024]{2,1,0:T(8,128)(4,1)} %copy-done.2, bf16[2,256,16,64]{1,3,2,0:T(8,128)(2,1)} %bitcast.192, bf16[2,1024,16,64]{1,3,2,0:T(8,128)(2,1)} %bitcast.189), kind=kOutput, calls=%fused_computation.1 | convolution fusion | flops 1115676672 | bytes 72941568 | tf_op jit(solution)/shard_map/rqhd,rkhd->rhqk/dot_general | solution.py:214
  387.4 28.0 %multiply_convert_fusion = bf16[2,16,256,1024]{3,2,1,0:T(8,128)(2,1)} fusion(f32[2,16,256,1024]{3,2,1,0:T(8,128)} %get-tuple-element.70, f32[2,16,256,1024]{3,2,1,0:T(8,128)} %get-tuple-element.64, f32[2,16,256]{2,1,0:T(8,128)S(1)} %copy-done.23, f32[2,16,256]{2,1,0:T(8,128)S(1)} %log_add_fusion, pred[2,256,1024]{2,1,0:T(8,128)(4,1)} %copy-done.2), kind=kLoop, calls=%fused_computation | loop fusion | flops 50331648 | bytes 84475904 | tf_op jit(solution)/shard_map/convert_element_type | solution.py:223
  417.8 18.1 %convolution_convert_fusion = bf16[2,16,64,1024]{3,2,1,0:T(8,128)(2,1)} fusion(bf16[2,256,16,64]{1,3,2,0:T(8,128)(2,1)} %bitcast.194, f32[2,16,256,1024]{3,2,1,0:T(8,128)} %get-tuple-element.64, f32[2,16,256]{2,1,0:T(8,128)S(1)} %log_add_fusion, pred[2,256,1024]{2,1,0:T(8,128)(4,1)} %copy-done.2), kind=kOutput, calls=%fused_computation.66 | convolution fusion | flops 1109393408 | bytes 39354368 | tf_op jit(solution)/shard_map/rhqk,rqhd->krhd/dot_general | solution.py:238
  435.8 6.3 copy.206
  442.2 11.3 %multiply_convert_fusion.1 = bf16[2,16,64,1024]{3,2,1,0:T(8,128)(2,1)} fusion(bf16[2,256,16,64]{1,3,2,0:T(8,128)(2,1)} %bitcast.187, bf16[2,16,256,1024]{3,2,1,0:T(8,128)(2,1)} %multiply_convert_fusion), kind=kOutput, calls=%fused_computation.42 | convolution fusion | flops 1077936128 | bytes 22020096 | tf_op jit(solution)/shard_map/rhqk,rqhd->krhd/dot_general | solution.py:235
  453.5 6.5 copy.205
  460.0 8.5 %pad_maximum_fusion = bf16[1024,2,2048]{2,0,1:T(8,128)(2,1)} fusion(bf16[1024,2,1024]{2,0,1:T(8,128)(2,1)} %copy.206, bf16[1024,2,1024]{2,0,1:T(8,128)(2,1)} %copy.205), kind=kLoop, calls=%fused_computation.31 | loop fusion | flops 16777216 | bytes 16777216 | tf_op jit(solution)/shard_map/concatenate | solution.py:242
  468.5 13.8 %fusion.181 = f32[2,16,64,256]{3,2,1,0:T(8,128)} fusion(bf16[2,1024,16,64]{1,3,2,0:T(8,128)(2,1)} %bitcast.183, bf16[2,16,256,1024]{3,2,1,0:T(8,128)(2,1)} %multiply_convert_fusion), kind=kOutput, calls=%fused_computation.225 | convolution fusion | flops 1073741824 | bytes 23068672 | tf_op jit(solution)/shard_map/rhqk,rkhd->rqhd/dot_general | solution.py:225
  489.9 40.9 %all-reduce = (f32[10,1024]{1,0:T(8,128)}, f32[512]{0:T(512)}, f32[2048]{0:T(1024)}) all-reduce(f32[10,1024]{1,0:T(8,128)S(1)} %fusion.182, f32[512]{0:T(512)S(1)} %get-tuple-element.73, f32[2048]{0:T(1024)S(1)} %reduce_sum.231), channel_id=1, replica_groups=mesh['seq'=4,'dp'=8] {'seq','dp'}, use_global_device_ids=true, to_apply=%region_23.24 | all-reduce | flops 12800 | bytes 102400 | tf_op jit(solution)/shard_map/psum | solution.py:275
  530.8 43.5 %all-reduce.4.cloned.1.call-done = (f32[1024,512]{0,1:T(8,128)}, f32[512,2048]{1,0:T(8,128)}) async-done(((f32[1024,512]{0,1:T(8,128)}, f32[512,2048]{1,0:T(8,128)}), (f32[1024,512]{0,1:T(8,128)}, f32[512,2048]{1,0:T(8,128)})) %all-reduce.4.cloned.1.call-update) | async-done | bytes 6291472 | tf_op jit(solution)/shard_map/psum | solution.py:275
  577.1 71.4 %reduce-scatter.2.cloned.1.call-done = bf16[256,2,2048]{2,0,1:T(8,128)(2,1)} async-done(((bf16[1024,2,2048]{2,0,1:T(8,128)(2,1)}), bf16[256,2,2048]{2,0,1:T(8,128)(2,1)}) %reduce-scatter.2.cloned.1.call-update) | async-done | bytes 2097168 | tf_op jit(solution)/shard_map/reduce_scatter | solution.py:241
  648.6 6.7 %fusion.63 = (f32[2,256]{1,0:T(2,128)S(1)}, f32[2,256,1024]{2,1,0:T(8,128)S(1)}) fusion(bf16[2,256,1024]{2,1,0:T(8,128)(2,1)S(1)} %copy-done.1, f32[2,256]{1,0:T(2,128)S(1)} %copy-done.30, f32[1024]{0:T(1024)S(1)} %copy-done.36, bf16[1024,3072]{1,0:T(8,128)(2,1)} %param.27, bf16[2,256,2048]{2,1,0:T(8,128)(2,1)} %bitcast.210, bf16[2,256,1024]{2,1,0:T(8,128)(2,1)} %copy.207), kind=kOutput, calls=%fused_computation.80 | convolution fusion | flops 3230137856 | bytes 12591104 | tf_op jit(solution)/shard_map/rcf,df->rcd/dot_general | solution.py:267
  (194 shorter events, 83.7 us)
Async XLA Ops:
  7.2 143.2 %copy-start = (bf16[1024,1024]{1,0:T(8,128)(2,1)S(1)}, bf16[1024,1024]{1,0:T(8,128)(2,1)}, u32[]{:S(2)}) copy-start(bf16[1024,1024]{1,0:T(8,128)(2,1)} %param.29) | copy-start | bytes 6291460
  7.2 74.2 %all-gather.3.cloned.1.call-start = ((), (), s32[]{:S(2)}) async-start(), calls=%async_computation.1 | async-start | bytes 10485760 | tf_op jit(solution)/shard_map/all_gather | solution.py:48
  20.3 215.9 %all-gather.5.cloned.1.call-start = ((), (), s32[]{:S(2)}) async-start(), calls=%async_computation.2 | async-start | bytes 10485760 | tf_op jit(solution)/shard_map/all_gather | solution.py:46
  25.6 169.8 %copy-start.16 = (bf16[10,16,64]{2,1,0:T(8,128)(2,1)}, bf16[10,16,64]{2,1,0:T(8,128)(2,1)S(1)}, u32[]{:S(2)}) copy-start(bf16[10,16,64]{2,1,0:T(8,128)(2,1)S(1)} %reshape.304) | copy-start | bytes 61444
  28.7 87.3 %copy-start.2 = (pred[2,256,1024]{2,1,0:T(8,128)(4,1)}, pred[2,256,1024]{2,1,0:T(8,128)(4,1)S(1)}, u32[]{:S(2)}) copy-start(pred[2,256,1024]{2,1,0:T(8,128)(4,1)S(1)} %broadcast_and_fusion) | copy-start | bytes 1572868
  99.8 15.9 %copy-start.7 = (f32[16,10,2,256]{3,1,2,0:T(8,128)S(1)}, f32[16,10,2,256]{3,1,2,0:T(8,128)}, u32[]{:S(2)}) copy-start(f32[16,10,2,256]{3,1,2,0:T(8,128)} %copy-done.6) | copy-start | bytes 983044
  132.9 17.5 %copy-start.1 = (bf16[2,256,1024]{2,1,0:T(8,128)(2,1)S(1)}, bf16[2,256,1024]{2,1,0:T(8,128)(2,1)}, u32[]{:S(2)}) copy-start(bf16[2,256,1024]{2,1,0:T(8,128)(2,1)} %param.21) | copy-start | bytes 3145732
  132.9 17.5 %copy-start.28 = (f32[1024]{0:T(1024)S(1)}, f32[1024]{0:T(1024)}, u32[]{:S(2)}) copy-start(f32[1024]{0:T(1024)} %param.30) | copy-start | bytes 12292
  150.5 13.6 %slice-start = ((s8[8388608]{0:T(1024)(128)(4,1)}), s8[4194304]{0:T(1024)(128)(4,1)S(1)}, s32[]{:S(2)}) async-start(s8[8388608]{0:T(1024)(128)(4,1)} %bitcast.206), calls=%async_computation.5 | async-start | bytes 8388608
  150.5 19.9 %slice-start.2 = ((s8[6291456]{0:T(1024)(128)(4,1)}), s8[4194304]{0:T(1024)(128)(4,1)S(1)}, s32[]{:S(2)}) async-start(s8[6291456]{0:T(1024)(128)(4,1)} %bitcast.208), calls=%async_computation.7 | async-start | bytes 8388608
  153.6 10.5 %slice-start.1 = ((s8[8388608]{0:T(1024)(128)(4,1)}), s8[4194304]{0:T(1024)(128)(4,1)S(1)}, s32[]{:S(2)}) async-start(s8[8388608]{0:T(1024)(128)(4,1)} %bitcast.206), calls=%async_computation.6 | async-start | bytes 8388608
  153.7 10.5 %copy-start.47 = (f32[1024]{0:T(1024)S(1)}, f32[1024]{0:T(1024)}, u32[]{:S(2)}) copy-start(f32[1024]{0:T(1024)} %param.36) | copy-start | bytes 12292
  153.7 16.7 %slice-start.3 = ((s8[6291456]{0:T(1024)(128)(4,1)}), s8[2097152]{0:T(1024)(128)(4,1)S(1)}, s32[]{:S(2)}) async-start(s8[6291456]{0:T(1024)(128)(4,1)} %bitcast.208), calls=%async_computation.8 | async-start | bytes 4194304
  164.2 6.3 copy-start.35
  164.2 6.3 copy-start.46
  164.2 6.2 copy-start.48
  177.7 396.6 %all-reduce.4.cloned.1.call-start = ((), (), s32[]{:S(2)}) async-start(), calls=%async_computation.4 | async-start | bytes 12582912 | tf_op jit(solution)/shard_map/psum | solution.py:275
  177.8 12.8 %copy-start.39 = (pred[2,256]{1,0:T(4,128)(4,1)}, pred[2,256]{1,0:T(4,128)(4,1)S(1)}, u32[]{:S(2)}) copy-start(pred[2,256]{1,0:T(4,128)(4,1)S(1)} %compare_and_fusion) | copy-start | bytes 1540
  254.6 16.0 %copy-start.3 = (pred[2,256,1024]{2,1,0:T(8,128)(4,1)S(1)}, pred[2,256,1024]{2,1,0:T(8,128)(4,1)}, u32[]{:S(2)}) copy-start(pred[2,256,1024]{2,1,0:T(8,128)(4,1)} %copy-done.2) | copy-start | bytes 1572868
  375.1 8.4 %copy-start.21 = (f32[10,512]{1,0:T(8,128)S(1)}, f32[10,512]{1,0:T(8,128)}, u32[]{:S(2)}) copy-start(f32[10,512]{1,0:T(8,128)} %copy-done.20) | copy-start | bytes 61444
  377.6 9.8 %copy-start.23 = (f32[2,16,256]{2,1,0:T(8,128)S(1)}, f32[2,16,256]{2,1,0:T(8,128)}, u32[]{:S(2)}) copy-start(f32[2,16,256]{2,1,0:T(8,128)} %copy-done.22) | copy-start | bytes 98308
  383.6 31.8 %copy-start.24 = (f32[10,512]{1,0:T(8,128)}, f32[10,512]{1,0:T(8,128)S(1)}, u32[]{:S(2)}) copy-start(f32[10,512]{1,0:T(8,128)S(1)} %get-tuple-element.74) | copy-start | bytes 61444
  387.4 28.0 %copy-start.27 = (bf16[10,1024]{1,0:T(8,128)(2,1)S(1)}, bf16[10,1024]{1,0:T(8,128)(2,1)}, u32[]{:S(2)}) copy-start(bf16[10,1024]{1,0:T(8,128)(2,1)} %param.37) | copy-start | bytes 61444
  417.7 230.9 %reduce-scatter.2.cloned.1.call-start = ((), (), s32[]{:S(2)}) async-start(), calls=%async_computation.3 | async-start | bytes 10485760 | tf_op jit(solution)/shard_map/reduce_scatter | solution.py:241
  468.5 13.8 %copy-start.15 = (bf16[2,16,256,10]{2,1,3,0:T(8,128)(2,1)S(1)}, bf16[2,16,256,10]{2,1,3,0:T(8,128)(2,1)}, u32[]{:S(2)}) copy-start(bf16[2,16,256,10]{2,1,3,0:T(8,128)(2,1)} %copy-done.14) | copy-start | bytes 491524
  468.5 13.8 %copy-start.17 = (bf16[10,16,64]{2,1,0:T(8,128)(2,1)S(1)}, bf16[10,16,64]{2,1,0:T(8,128)(2,1)}, u32[]{:S(2)}) copy-start(bf16[10,16,64]{2,1,0:T(8,128)(2,1)} %copy-done.16) | copy-start | bytes 61444
  485.4 163.1 %copy-start.30 = (f32[2,256]{1,0:T(2,128)S(1)}, f32[2,256]{1,0:T(2,128)}, u32[]{:S(2)}) copy-start(f32[2,256]{1,0:T(2,128)} %copy-done.29) | copy-start | bytes 6148
  485.4 163.1 %copy-start.36 = (f32[1024]{0:T(1024)S(1)}, f32[1024]{0:T(1024)}, u32[]{:S(2)}) copy-start(f32[1024]{0:T(1024)} %param.25) | copy-start | bytes 12292
  648.6 6.8 %copy-start.32 = (f32[2,256]{1,0:T(2,128)S(1)}, f32[2,256]{1,0:T(2,128)}, u32[]{:S(2)}) copy-start(f32[2,256]{1,0:T(2,128)} %copy-done.31) | copy-start | bytes 6148
  648.6 6.8 %copy-start.34 = (f32[2,256]{1,0:T(2,128)S(1)}, f32[2,256]{1,0:T(2,128)}, u32[]{:S(2)}) copy-start(f32[2,256]{1,0:T(2,128)} %copy-done.33) | copy-start | bytes 6148
  648.6 7.5 %copy-start.19 = (bf16[2,256,1024]{2,1,0:T(8,128)(2,1)S(1)}, bf16[2,256,1024]{2,1,0:T(8,128)(2,1)}, u32[]{:S(2)}) copy-start(bf16[2,256,1024]{2,1,0:T(8,128)(2,1)} %param.22) | copy-start | bytes 3145732
  648.6 7.5 %copy-start.41 = (pred[2,256]{1,0:T(4,128)(4,1)S(1)}, pred[2,256]{1,0:T(4,128)(4,1)}, u32[]{:S(2)}) copy-start(pred[2,256]{1,0:T(4,128)(4,1)} %copy-done.39) | copy-start | bytes 1540
  (26 other events, 76.9 us)
Sparse Core Ops, SparseCore 0:
  20.4 60.9 all-gather.2
  177.8 58.2 all-gather.4
  417.8 156.4 all-reduce.3
  576.9 71.6 reduce-scatter.1
where the time goes:
time: 674 us; the launch traced here: 669 us
  matrix products  241 us (36%)
  waiting for transfers between devices  207 us (31%)
  local copies, waits for them, and re-layouts  83.7 us (12%)
  other arithmetic  81.4 us (12%)
  blocking collectives  40.9 us (6%)
  between operations  14.8 us (2%)
    all_gather x2, waiting for transfers between devices, block_forward(): row_keyval = lax.all_gather(local_keyval, 'seq', axis=1, tiled=True)  91.8 us
    reduce_scatter x1, waiting for transfers between devices, per_device(): lax.psum_scatter(jnp.concatenate([grad_keys.reshape(tok_count * lax.axis_...  71.4 us
    psum x1, waiting for transfers between devices, per_device(): lax.psum((grad_table, grad_lift, grad_liftbias, grad_fan, grad_fanbias),...  43.5 us
    psum x1, blocking collectives, per_device(): lax.psum((grad_table, grad_lift, grad_liftbias, grad_fan, grad_fanbias),...  40.9 us
    dot_general x2, matrix products, block_forward(): jnp.einsum('rhqk,rkhd->rqhd', rounded, row_values, preferred_element_type...  34.5 us
    dot_general x2, matrix products, block_forward(): jnp.einsum('rqhd,rkhd->rhqk', queries, row_keys, preferred_element_type=j...  31.8 us
    reduce_sum x2, other arithmetic, block_forward(): jnp.sum(jnp.exp(scores - highest), axis=-1, keepdims=True)  29.7 us
    convert_element_type x1, other arithmetic, per_device(): grad_scores = (weights * (grad_weights - inner_sum)).astype(jnp.bfloat16)  28 us
  transfers between devices with their start and end apart: 4, of which 4 were waited for; matrix products, arithmetic and copies ran while one was open for 15% of the time, Pallas kernels for 0%

commit v1 on v0

--- a/solution.py
+++ b/solution.py
@@ -273,7 +273,7 @@
         prefix_grad, prefix_table, lift_weight, fan_weight, lifted, lifted_low
     )
     grad_table, grad_lift, grad_liftbias, grad_fan, grad_fanbias = lax.psum(
-        (grad_table, grad_lift, grad_liftbias, grad_fan, grad_fanbias), ("seq", "dp")
+        lax.psum((grad_table, grad_lift, grad_liftbias, grad_fan, grad_fanbias), "dp"), "seq"
     )
     return (activations, input_grad, grad_table, grad_lift, grad_liftbias, grad_fan, grad_fanbias)
 

time: 674 us -> 822 us (1.22)
  waiting for transfers between devices: 207 us -> 353 us
  blocking collectives: 40.9 us -> 49.8 us
    psum x1, waiting for transfers between devices: 43.5 us -> 184 us  [per_device(): lax.psum((grad_table, grad_lift, grad_liftbias, grad_fan, grad_fanbias),...]
    psum x0 -> x1, blocking collectives: none -> 13.7 us  [per_device(): lax.psum(lax.psum((grad_table, grad_lift, grad_liftbias, grad_fan, grad_f...]
  transfers between devices with their start and end apart: 4 -> 5, of which waited for: 4 -> 5; matrix products, arithmetic and copies ran while one was open for 15% -> 15% of each run, Pallas kernels for 0% -> 0%
where the time goes in v1:
time: 822 us; the launch traced here: 817 us
  waiting for transfers between devices  353 us (43%)
  matrix products  237 us (29%)
  other arithmetic  81.5 us (10%)
  local copies, waits for them, and re-layouts  81.1 us (10%)
  blocking collectives  49.8 us (6%)
  between operations  14.8 us (2%)
    psum x1, waiting for transfers between devices, per_device(): lax.psum((grad_table, grad_lift, grad_liftbias, grad_fan, grad_fanbias),...  184 us
    all_gather x2, waiting for transfers between devices, block_forward(): row_keyval = lax.all_gather(local_keyval, 'seq', axis=1, tiled=True)  91.8 us
    reduce_scatter x1, waiting for transfers between devices, per_device(): lax.psum_scatter(jnp.concatenate([grad_keys.reshape(tok_count * lax.axis_...  71.7 us
    psum x1, blocking collectives, per_device(): lax.psum((grad_table, grad_lift, grad_liftbias, grad_fan, grad_fanbias),...  36.1 us
    dot_general x2, matrix products, block_forward(): jnp.einsum('rhqk,rkhd->rqhd', rounded, row_values, preferred_element_type...  34.5 us
    dot_general x2, matrix products, block_forward(): jnp.einsum('rqhd,rkhd->rhqk', queries, row_keys, preferred_element_type=j...  31.8 us
    reduce_sum x2, other arithmetic, block_forward(): jnp.sum(jnp.exp(scores - highest), axis=-1, keepdims=True)  29.7 us
    convert_element_type x1, other arithmetic, per_device(): grad_scores = (weights * (grad_weights - inner_sum)).astype(jnp.bfloat16)  28.4 us
  transfers between devices with their start and end apart: 5, of which 5 were waited for; matrix products, arithmetic and copies ran while one was open for 15% of the time, Pallas kernels for 0%

profile of v1, /device:TPU:0, one launch (start us, length us, event | category | flops | bytes accessed | tf_op | source)
XLA Modules:
  0.0 817.1 jit_solution(14372100279311023988)
XLA Ops:
  10.5 6.6 add_convert_fusion.1
  28.7 52.7 %all-gather.3.cloned.1.call-done = bf16[2,1024,2048]{2,1,0:T(8,128)(2,1)} async-done(((bf16[2,256,2048]{2,1,0:T(8,128)(2,1)}), bf16[2,1024,2048]{2,1,0:T(8,128)(2,1)}) %all-gather.3.cloned.1.call-update) | async-done | bytes 8388624 | tf_op jit(solution)/shard_map/all_gather | solution.py:48
  81.4 6.0 fusion.174
  87.4 6.2 copy.171
  93.6 6.2 copy.173
  99.8 15.9 %fusion = (f32[2,16,256]{2,1,0:T(8,128)S(1)}, f32[2,16,256,1024]{3,2,1,0:T(8,128)}) fusion(pred[2,256,1024]{2,1,0:T(8,128)(4,1)S(1)} %broadcast_and_fusion, bf16[2,256,16,64]{1,3,2,0:T(8,128)(2,1)} %bitcast.197, bf16[2,1024,16,64]{1,3,2,0:T(8,128)(2,1)} %bitcast.195), kind=kOutput, calls=%fused_computation.8 | convolution fusion | flops 1098899456 | bytes 39354368 | tf_op jit(solution)/shard_map/rqhd,rkhd->rhqk/dot_general | solution.py:55
  116.0 14.9 %exponential_reduce_fusion.1 = f32[2,16,256]{2,1,0:T(8,128)S(1)} fusion(f32[2,16,256,1024]{3,2,1,0:T(8,128)} %get-tuple-element.65, f32[2,16,256]{2,1,0:T(8,128)S(1)} %max.22, pred[2,256,1024]{2,1,0:T(8,128)(4,1)S(1)} %broadcast_and_fusion), kind=kLoop, calls=%fused_computation.6 | loop fusion | flops 33546240 | bytes 34144256 | tf_op jit(solution)/shard_map/reduce_sum | solution.py:70
  132.9 17.5 %fusion.74 = bf16[2,256,16,64]{1,3,2,0:T(8,128)(2,1)} fusion(f32[16,64,2,256]{3,1,0,2:T(8,128)} %fusion.137, bf16[2,1024,16,64]{1,3,2,0:T(8,128)(2,1)} %bitcast.198, f32[2,16,256,1024]{3,2,1,0:T(8,128)} %get-tuple-element.65, f32[2,16,256]{2,1,0:T(8,128)S(1)} %log_add_fusion.1, pred[2,256,1024]{2,1,0:T(8,128)(4,1)} %copy-done.3), kind=kOutput, calls=%fused_computation.94 | convolution fusion | flops 1108344832 | bytes 41451520 | tf_op jit(solution)/shard_map/rhqk,rkhd->rqhd/dot_general | solution.py:78
  153.7 10.4 %fusion.19 = bf16[2,256,4096]{2,1,0:T(8,128)(2,1)S(1)} fusion(bf16[1024,4096]{1,0:T(8,128)(2,1)} %param.33, f32[4096]{0:T(1024)S(1)} %copy-done.46, f32[2,256,1024]{2,1,0:T(8,128)S(1)} %get-tuple-element.67, f32[1024]{0:T(1024)S(1)} %copy-done.50, f32[1024]{0:T(1024)S(1)} %copy-done.39, f32[2,256]{1,0:T(2,128)S(1)} %add_rsqrt_fusion, ...), kind=kOutput, calls=%fused_computation.30 | convolution fusion | flops 4318560256 | bytes 14708736 | tf_op jit(solution)/shard_map/dot_general | solution.py:91
  164.2 5.5 add_convert_fusion.3
  177.9 12.7 %fusion.20 = f32[2,256,4096]{2,1,0:T(8,128)} fusion(bf16[4096,1024]{1,0:T(8,128)(2,1)} %param.35, bf16[2,256,1024]{2,1,0:T(8,128)(2,1)} %param.22, pred[2,256]{1,0:T(4,128)(4,1)S(1)} %compare_and_fusion), kind=kOutput, calls=%fused_computation.32 | convolution fusion | flops 4295491584 | bytes 17826304 | tf_op jit(solution)/shard_map/rcd,fd->rcf/dot_general | solution.py:197
  197.0 39.1 %all-gather.5.cloned.1.call-done = bf16[2,1024,2048]{2,1,0:T(8,128)(2,1)} async-done(((bf16[2,256,2048]{2,1,0:T(8,128)(2,1)}), bf16[2,1024,2048]{2,1,0:T(8,128)(2,1)}) %all-gather.5.cloned.1.call-update) | async-done | bytes 8388624 | tf_op jit(solution)/shard_map/all_gather | solution.py:46
  236.2 6.0 fusion.173
  242.2 6.2 copy.186
  248.4 6.2 copy.184
  254.6 15.9 %fusion.1 = (f32[2,16,256]{2,1,0:T(8,128)S(1)}, f32[2,16,256,1024]{3,2,1,0:T(8,128)}) fusion(pred[2,256,1024]{2,1,0:T(8,128)(4,1)} %copy-done.3, bf16[2,256,16,64]{1,3,2,0:T(8,128)(2,1)} %bitcast.185, bf16[2,1024,16,64]{1,3,2,0:T(8,128)(2,1)} %bitcast.182), kind=kOutput, calls=%fused_computation.9 | convolution fusion | flops 1098899456 | bytes 39354368 | tf_op jit(solution)/shard_map/rqhd,rkhd->rhqk/dot_general | solution.py:55
  270.6 14.9 %exponential_reduce_fusion = f32[2,16,256]{2,1,0:T(8,128)S(1)} fusion(f32[2,16,256,1024]{3,2,1,0:T(8,128)} %get-tuple-element.69, f32[2,16,256]{2,1,0:T(8,128)S(1)} %max.23, pred[2,256,1024]{2,1,0:T(8,128)(4,1)S(1)} %copy-done.4), kind=kLoop, calls=%fused_computation.3 | loop fusion | flops 33546240 | bytes 34144256 | tf_op jit(solution)/shard_map/reduce_sum | solution.py:70
  286.2 17.0 %fusion.141 = f32[2,16,64,256]{3,2,1,0:T(8,128)} fusion(bf16[2,1024,16,64]{1,3,2,0:T(8,128)(2,1)} %bitcast.188, f32[2,16,256,1024]{3,2,1,0:T(8,128)} %get-tuple-element.69, f32[2,16,256]{2,1,0:T(8,128)S(1)} %log_add_fusion, pred[2,256,1024]{2,1,0:T(8,128)(4,1)} %copy-done.3), kind=kOutput, calls=%fused_computation.169 | convolution fusion | flops 1107296256 | bytes 40402944 | tf_op jit(solution)/shard_map/rhqk,rkhd->rqhd/dot_general | solution.py:78
  309.0 23.9 %multiply_reduce_fusion.1 = (f32[2,256]{1,0:T(2,128)}, f32[2,256,1024]{2,1,0:T(8,128)}) fusion(f32[2,256,1024]{2,1,0:T(8,128)} %copy-done.8, f32[2,256]{1,0:T(2,128)S(1)} %broadcast_multiply_fusion, f32[1024]{0:T(1024)} %param.31, bf16[1024,4096]{1,0:T(8,128)(2,1)} %param.33, f32[2,256,4096]{2,1,0:T(8,128)} %fusion.20, f32[4096]{0:T(1024)} %param.34, ...), kind=kOutput, calls=%fused_computation.97 | convolution fusion | flops 8638693376 | bytes 21002240 | tf_op jit(solution)/shard_map/rcf,df->rcd/dot_general | solution.py:202
  344.1 27.3 %multiply_reduce_fusion = (f32[2,16,256]{2,1,0:T(8,128)}, f32[2,16,256,1024]{3,2,1,0:T(8,128)}) fusion(f32[2,16,256,1024]{3,2,1,0:T(8,128)} %get-tuple-element.69, f32[2,16,256]{2,1,0:T(8,128)S(1)} %log_add_fusion, pred[2,256,1024]{2,1,0:T(8,128)(4,1)S(1)} %copy-done.5, bf16[2,256,16,64]{1,3,2,0:T(8,128)(2,1)} %bitcast.192, ...), kind=kOutput, calls=%fused_computation.1 | convolution fusion | flops 1115676672 | bytes 72941568 | tf_op jit(solution)/shard_map/rqhd,rkhd->rhqk/dot_general | solution.py:214
  387.3 28.4 %multiply_convert_fusion = bf16[2,16,256,1024]{3,2,1,0:T(8,128)(2,1)} fusion(f32[2,16,256,1024]{3,2,1,0:T(8,128)} %get-tuple-element.75, f32[2,16,256,1024]{3,2,1,0:T(8,128)} %get-tuple-element.69, f32[2,16,256]{2,1,0:T(8,128)S(1)} %add.290, f32[2,16,256]{2,1,0:T(8,128)S(1)} %log_add_fusion, pred[2,256,1024]{2,1,0:T(8,128)(4,1)S(1)} %copy-done.5), kind=kLoop, calls=%fused_computation | loop fusion | flops 50331648 | bytes 84475904 | tf_op jit(solution)/shard_map/convert_element_type | solution.py:223
  415.8 184.3 %all-reduce.7.cloned.1.call-done = (f32[1024,512]{0,1:T(8,128)}, f32[512,2048]{1,0:T(8,128)}) async-done(((f32[1024,512]{0,1:T(8,128)}, f32[512,2048]{1,0:T(8,128)}), (f32[1024,512]{0,1:T(8,128)}, f32[512,2048]{1,0:T(8,128)})) %all-reduce.7.cloned.1.call-update) | async-done | bytes 6291472 | tf_op jit(solution)/shard_map/psum | solution.py:276
  600.2 18.3 %convolution_convert_fusion = bf16[2,16,64,1024]{3,2,1,0:T(8,128)(2,1)} fusion(bf16[2,256,16,64]{1,3,2,0:T(8,128)(2,1)} %bitcast.194, f32[2,16,256,1024]{3,2,1,0:T(8,128)} %get-tuple-element.69, f32[2,16,256]{2,1,0:T(8,128)S(1)} %log_add_fusion, pred[2,256,1024]{2,1,0:T(8,128)(4,1)S(1)} %copy-done.5), kind=kOutput, calls=%fused_computation.66 | convolution fusion | flops 1109393408 | bytes 39354368 | tf_op jit(solution)/shard_map/rhqk,rqhd->krhd/dot_general | solution.py:238
  618.5 6.3 copy.206
  624.8 10.9 %multiply_convert_fusion.1 = bf16[2,16,64,1024]{3,2,1,0:T(8,128)(2,1)} fusion(bf16[2,256,16,64]{1,3,2,0:T(8,128)(2,1)S(1)} %bitcast.187, bf16[2,16,256,1024]{3,2,1,0:T(8,128)(2,1)} %multiply_convert_fusion), kind=kOutput, calls=%fused_computation.42 | convolution fusion | flops 1077936128 | bytes 22020096 | tf_op jit(solution)/shard_map/rhqk,rqhd->krhd/dot_general | solution.py:235
  635.7 6.5 copy.205
  642.2 8.2 pad_maximum_fusion
  650.4 12.5 %fusion.181 = f32[2,16,64,256]{3,2,1,0:T(8,128)S(1)} fusion(bf16[2,1024,16,64]{1,3,2,0:T(8,128)(2,1)} %bitcast.183, bf16[2,16,256,1024]{3,2,1,0:T(8,128)(2,1)} %multiply_convert_fusion), kind=kOutput, calls=%fused_computation.225 | convolution fusion | flops 1073741824 | bytes 23068672 | tf_op jit(solution)/shard_map/rhqk,rkhd->rqhd/dot_general | solution.py:225
  668.2 36.1 %all-reduce = (f32[10,1024]{1,0:T(8,128)S(1)}, f32[512]{0:T(512)S(1)}, f32[2048]{0:T(1024)S(1)}) all-reduce(f32[10,1024]{1,0:T(8,128)S(1)} %fusion.182, f32[512]{0:T(512)S(1)} %get-tuple-element.78, f32[2048]{0:T(1024)S(1)} %reduce_sum.231), channel_id=1, replica_groups=mesh['seq'=4,'dp'=8] {'dp'}, use_global_device_ids=true, to_apply=%region_23.24 | all-reduce | flops 12800 | bytes 102400 | tf_op jit(solution)/shard_map/psum | solution.py:276
  704.3 13.7 %all-reduce.2 = (f32[10,1024]{1,0:T(8,128)}, f32[512]{0:T(512)}, f32[2048]{0:T(1024)}) all-reduce(f32[10,1024]{1,0:T(8,128)S(1)} %get-tuple-element.44, f32[512]{0:T(512)S(1)} %get-tuple-element.45, f32[2048]{0:T(1024)S(1)} %get-tuple-element.46), channel_id=1, replica_groups=mesh['seq'=4,'dp'=8] {'seq'}, use_global_device_ids=true, to_apply=%region_24.25 | all-reduce | flops 12800 | bytes 102400 | tf_op jit(solution)/shard_map/psum | solution.py:275
  725.5 71.7 %reduce-scatter.2.cloned.1.call-done = bf16[256,2,2048]{2,0,1:T(8,128)(2,1)} async-done(((bf16[1024,2,2048]{2,0,1:T(8,128)(2,1)}), bf16[256,2,2048]{2,0,1:T(8,128)(2,1)}) %reduce-scatter.2.cloned.1.call-update) | async-done | bytes 2097168 | tf_op jit(solution)/shard_map/reduce_scatter | solution.py:241
  797.3 6.5 fusion.63
  (200 shorter events, 87.6 us)
Async XLA Ops:
  7.2 143.3 %copy-start = (bf16[1024,1024]{1,0:T(8,128)(2,1)S(1)}, bf16[1024,1024]{1,0:T(8,128)(2,1)}, u32[]{:S(2)}) copy-start(bf16[1024,1024]{1,0:T(8,128)(2,1)} %param.29) | copy-start | bytes 6291460
  7.2 74.2 %all-gather.3.cloned.1.call-start = ((), (), s32[]{:S(2)}) async-start(), calls=%async_computation.1 | async-start | bytes 10485760 | tf_op jit(solution)/shard_map/all_gather | solution.py:48
  20.3 215.9 %all-gather.5.cloned.1.call-start = ((), (), s32[]{:S(2)}) async-start(), calls=%async_computation.2 | async-start | bytes 10485760 | tf_op jit(solution)/shard_map/all_gather | solution.py:46
  25.6 169.8 %copy-start.20 = (bf16[10,16,64]{2,1,0:T(8,128)(2,1)}, bf16[10,16,64]{2,1,0:T(8,128)(2,1)S(1)}, u32[]{:S(2)}) copy-start(bf16[10,16,64]{2,1,0:T(8,128)(2,1)S(1)} %reshape.304) | copy-start | bytes 61444
  28.7 87.3 %copy-start.3 = (pred[2,256,1024]{2,1,0:T(8,128)(4,1)}, pred[2,256,1024]{2,1,0:T(8,128)(4,1)S(1)}, u32[]{:S(2)}) copy-start(pred[2,256,1024]{2,1,0:T(8,128)(4,1)S(1)} %broadcast_and_fusion) | copy-start | bytes 1572868
  99.8 15.9 %copy-start.11 = (f32[16,10,2,256]{3,1,2,0:T(8,128)S(1)}, f32[16,10,2,256]{3,1,2,0:T(8,128)}, u32[]{:S(2)}) copy-start(f32[16,10,2,256]{3,1,2,0:T(8,128)} %copy-done.10) | copy-start | bytes 983044
  132.9 17.5 %copy-start.2 = (bf16[2,256,1024]{2,1,0:T(8,128)(2,1)S(1)}, bf16[2,256,1024]{2,1,0:T(8,128)(2,1)}, u32[]{:S(2)}) copy-start(bf16[2,256,1024]{2,1,0:T(8,128)(2,1)} %param.21) | copy-start | bytes 3145732
  132.9 17.5 %copy-start.29 = (f32[1024]{0:T(1024)S(1)}, f32[1024]{0:T(1024)}, u32[]{:S(2)}) copy-start(f32[1024]{0:T(1024)} %param.30) | copy-start | bytes 12292
  150.5 13.7 %slice-start = ((s8[8388608]{0:T(1024)(128)(4,1)}), s8[4194304]{0:T(1024)(128)(4,1)S(1)}, s32[]{:S(2)}) async-start(s8[8388608]{0:T(1024)(128)(4,1)} %bitcast.206), calls=%async_computation.6 | async-start | bytes 8388608
  150.5 19.9 %slice-start.2 = ((s8[6291456]{0:T(1024)(128)(4,1)}), s8[4194304]{0:T(1024)(128)(4,1)S(1)}, s32[]{:S(2)}) async-start(s8[6291456]{0:T(1024)(128)(4,1)} %bitcast.208), calls=%async_computation.8 | async-start | bytes 8388608
  153.7 10.5 %slice-start.1 = ((s8[8388608]{0:T(1024)(128)(4,1)}), s8[4194304]{0:T(1024)(128)(4,1)S(1)}, s32[]{:S(2)}) async-start(s8[8388608]{0:T(1024)(128)(4,1)} %bitcast.206), calls=%async_computation.7 | async-start | bytes 8388608
  153.7 10.5 %copy-start.48 = (f32[1024]{0:T(1024)S(1)}, f32[1024]{0:T(1024)}, u32[]{:S(2)}) copy-start(f32[1024]{0:T(1024)} %param.36) | copy-start | bytes 12292
  153.7 16.7 %slice-start.3 = ((s8[6291456]{0:T(1024)(128)(4,1)}), s8[2097152]{0:T(1024)(128)(4,1)S(1)}, s32[]{:S(2)}) async-start(s8[6291456]{0:T(1024)(128)(4,1)} %bitcast.208), calls=%async_computation.9 | async-start | bytes 4194304
  164.2 6.3 copy-start.36
  164.2 6.3 copy-start.47
  164.2 6.2 copy-start.49
  177.7 422.4 %all-reduce.7.cloned.1.call-start = ((), (), s32[]{:S(2)}) async-start(), calls=%async_computation.4 | async-start | bytes 12582912 | tf_op jit(solution)/shard_map/psum | solution.py:276
  177.9 12.8 %copy-start.40 = (pred[2,256]{1,0:T(4,128)(4,1)}, pred[2,256]{1,0:T(4,128)(4,1)S(1)}, u32[]{:S(2)}) copy-start(pred[2,256]{1,0:T(4,128)(4,1)S(1)} %compare_and_fusion) | copy-start | bytes 1540
  254.6 16.0 %copy-start.4 = (pred[2,256,1024]{2,1,0:T(8,128)(4,1)S(1)}, pred[2,256,1024]{2,1,0:T(8,128)(4,1)}, u32[]{:S(2)}) copy-start(pred[2,256,1024]{2,1,0:T(8,128)(4,1)} %copy-done.3) | copy-start | bytes 1572868
  344.1 31.4 %copy-start.6 = (bf16[2,256,1024]{1,2,0:T(8,128)(2,1)S(1)}, bf16[2,256,1024]{1,2,0:T(8,128)(2,1)}, u32[]{:S(2)}) copy-start(bf16[2,256,1024]{1,2,0:T(8,128)(2,1)} %copy.185) | copy-start | bytes 3145732
  375.6 9.3 %copy-start.28 = (bf16[10,1024]{1,0:T(8,128)(2,1)S(1)}, bf16[10,1024]{1,0:T(8,128)(2,1)}, u32[]{:S(2)}) copy-start(bf16[10,1024]{1,0:T(8,128)(2,1)} %param.37) | copy-start | bytes 61444
  380.3 7.0 copy-start.25
  387.3 335.4 %all-reduce.9.cloned.1.call-start = ((), (), s32[]{:S(2)}) async-start(), calls=%async_computation.5 | async-start | bytes 12582912 | tf_op jit(solution)/shard_map/psum | solution.py:275
  600.1 197.1 %reduce-scatter.2.cloned.1.call-start = ((), (), s32[]{:S(2)}) async-start(), calls=%async_computation.3 | async-start | bytes 10485760 | tf_op jit(solution)/shard_map/reduce_scatter | solution.py:241
  650.4 12.5 %copy-start.19 = (bf16[2,16,256,10]{2,1,3,0:T(8,128)(2,1)S(1)}, bf16[2,16,256,10]{2,1,3,0:T(8,128)(2,1)}, u32[]{:S(2)}) copy-start(bf16[2,16,256,10]{2,1,3,0:T(8,128)(2,1)} %copy-done.18) | copy-start | bytes 491524
  650.4 12.5 %copy-start.21 = (bf16[10,16,64]{2,1,0:T(8,128)(2,1)S(1)}, bf16[10,16,64]{2,1,0:T(8,128)(2,1)}, u32[]{:S(2)}) copy-start(bf16[10,16,64]{2,1,0:T(8,128)(2,1)} %copy-done.20) | copy-start | bytes 61444
  664.4 132.8 %copy-start.31 = (f32[2,256]{1,0:T(2,128)S(1)}, f32[2,256]{1,0:T(2,128)}, u32[]{:S(2)}) copy-start(f32[2,256]{1,0:T(2,128)} %copy-done.30) | copy-start | bytes 6148
  664.5 132.8 %copy-start.37 = (f32[1024]{0:T(1024)S(1)}, f32[1024]{0:T(1024)}, u32[]{:S(2)}) copy-start(f32[1024]{0:T(1024)} %param.25) | copy-start | bytes 12292
  797.2 6.5 copy-start.33
  797.2 6.6 copy-start.35
  797.2 7.3 copy-start.23
  797.2 7.3 copy-start.42
  (28 other events, 81.7 us)
Sparse Core Ops, SparseCore 0:
  20.4 60.9 all-gather.2
  177.9 58.2 all-gather.4
  387.4 212.6 all-reduce.6
  602.5 120.0 all-reduce.8
  725.2 71.9 reduce-scatter.1
